TPU v7x, 128 devices: a whole 4x4x4 slice. The times are simulated.
128 devices in a mesh: gx: 16 (over y, x), gy: 8 (over z, core).
Axes of the slice: x: 4, y: 4, z: 4, core: 2. Of those that a mesh axis runs over, the one named last changes fastest.
Arguments:
- tiles: bfloat16 [3, 8, 768, 8704], P(None, None, 'gy', 'gx'), may hold values from 0.099609375 to 4
- offsets: int32 [8, 16, 2], P('gy', 'gx'), may hold values from 0 to 32, as said below
- psf: float32 [3, 3, 31], replicated, may hold values from 0.05 to 1
Outputs:
- restored: float32 [3, 8, 512, 8192], P(None, None, 'gy', 'gx')
- level_one: float32 [3, 4, 256, 4096], P(None, None, 'gy', 'gx')
- level_two: float32 [3, 2, 128, 2048], P(None, None, 'gy', 'gx')
Inputs may be any that keep to these rules, and one draw needn't show every extreme that they name: offsets[j, i, 0] is 0 for j = 0 and 32 for j = 7; offsets[j, i, 1] is 0 for i = 0 and 32 for i = 15.
All inputs are finite; a program needn't handle non-finite values.
Results may differ from a plain program's by a relative error of at most 0.0015.
Values may be sent and summed in bfloat16 or wider, within the bound.
A program may use at most 128 MiB of HBM per device.

v0:
```python
import jax
import jax.numpy as jnp
import numpy as np
from jax import lax
from jax.experimental import pallas as pl
from jax.experimental.pallas import tpu as pltpu
from jax.sharding import PartitionSpec as P

MESH = pl.DeviceIdType.MESH
F32 = jnp.float32
BF16 = jnp.bfloat16

CH, NZ, ROWS, COLS = 3, 8, 64, 512
MARGIN = 32
TROWS, TCOLS = ROWS + MARGIN, COLS + MARGIN
TAPS, HALF = 31, 15
ITERS = 2
STEPS = 2 * ITERS + 1
EDGE = 16
LANES = 128
OWN, STRIP = NZ * ROWS, NZ * EDGE
ALL = OWN + 2 * STRIP

GAUSS = np.array([1.0, 4.0, 6.0, 4.0, 1.0]) / 16.0


def _shrink(size_out, inputs):
    tap = np.asarray(inputs)[None, :] - 2 * np.arange(size_out)[:, None] + 2
    return np.where((tap >= 0) & (tap < 5), GAUSS[np.clip(tap, 0, 4)], 0.0)


def _shrink_twice(size_out, inputs, low_edge, high_edge):
    mid = np.arange(-2, 2 * size_out + 1)
    first = np.asarray(inputs)[None, :] - 2 * mid[:, None] + 2
    first = np.where((first >= 0) & (first < 5), GAUSS[np.clip(first, 0, 4)], 0.0)
    second = mid[None, :] - 2 * np.arange(size_out)[:, None] + 2
    second = np.where((second >= 0) & (second < 5), GAUSS[np.clip(second, 0, 4)], 0.0)
    keep = np.ones(mid.size)
    if low_edge:
        keep[mid < 0] = 0.0
    if high_edge:
        keep[mid >= 2 * size_out] = 0.0
    return second @ (keep[:, None] * first)


def _pyramid_rows():
    z_in = np.arange(NZ)
    z_one = _shrink(NZ // 2, z_in)
    z_two = _shrink(NZ // 4, np.arange(NZ // 2)) @ z_one
    parts = []
    for low, high in ((False, False), (True, False), (False, True)):
        blocks = []
        for coords, live in (
            (np.arange(ROWS), True),
            (np.arange(-EDGE, 0), not low),
            (np.arange(ROWS, ROWS + EDGE), not high),
        ):
            one = _shrink(ROWS // 2, coords) * live
            two = _shrink_twice(ROWS // 4, coords, low, high) * live
            blocks.append(np.concatenate([np.kron(z_one, one), np.kron(z_two, two)], axis=0))
        parts.append(np.concatenate(blocks, axis=1))
    return np.stack(parts).astype(jnp.bfloat16)


def _pyramid_cols():
    lane = np.arange(LANES)
    far = 10 * COLS
    edge = np.where(lane >= LANES - EDGE, lane - LANES, np.where(lane < EDGE, COLS + lane, far))
    coords = np.concatenate([edge, np.arange(COLS)])
    one = _shrink(COLS // 2, coords).T
    twos = [
        _shrink_twice(COLS // 4, coords, low, high).T
        for low, high in ((False, False), (True, False), (False, True))
    ]
    return one.astype(jnp.bfloat16), np.stack(twos).astype(jnp.bfloat16)


def _iota(shape, dim):
    return lax.broadcasted_iota(jnp.int32, shape, dim)


def _kernel(
    sizes,
    offsets_ref,
    psf_ref,
    tiles_ref,
    prow_ref,
    pone_ref,
    ptwo_ref,
    est_ref,
    one_ref,
    two_ref,
    shifted,
    own,
    low_send,
    low_recv,
    side_send,
    side_recv,
    info_send,
    info_recv,
    recip,
    joined,
    cur,
    top_recv,
    bot_recv,
    pack_right,
    pack_left,
    left_recv,
    right_recv,
    edge,
    spread,
    mat_x,
    mat_zy,
    join_send_sem,
    join_recv_sem,
    info_send_sem,
    info_recv_sem,
    send_sem,
    recv_sem,
):
    n_gx, n_gy = sizes
    gx, gy = lax.axis_index("gx"), lax.axis_index("gy")
    east, west = lax.rem(gx + 1, n_gx), lax.rem(gx + n_gx - 1, n_gx)
    south, north = lax.rem(gy + 1, n_gy), lax.rem(gy + n_gy - 1, n_gy)

    def at(x, y):
        return {"gx": x, "gy": y}

    around = [
        at(east, gy),
        at(west, gy),
        at(gx, south),
        at(gx, north),
        at(east, south),
        at(east, north),
        at(west, south),
        at(west, north),
    ]
    barrier = pltpu.get_barrier_semaphore()
    for place in around:
        pl.semaphore_signal(barrier, inc=1, device_id=place, device_id_type=MESH)
    pl.semaphore_wait(barrier, len(around))

    def remote(src, dst, send, recv, place):
        return pltpu.make_async_remote_copy(
            src_ref=src, dst_ref=dst, send_sem=send, recv_sem=recv, device_id=place, device_id_type=MESH
        )

    def join_copies(c):
        return [
            remote(low_send.at[c], low_recv.at[c], join_send_sem.at[c, 0], join_recv_sem.at[c, 0], around[2]),
            remote(side_send.at[c, 0], side_recv.at[c, 0], join_send_sem.at[c, 1], join_recv_sem.at[c, 1], around[0]),
            remote(side_send.at[c, 1], side_recv.at[c, 1], join_send_sem.at[c, 2], join_recv_sem.at[c, 2], around[4]),
        ]

    def info_copies():
        return [
            remote(info_send, info_recv.at[n], info_send_sem.at[n], info_recv_sem.at[n], around[k])
            for n, k in enumerate((0, 2, 4))
        ]

    def halo_copies(s, c):
        first, last = pl.ds(0, EDGE), pl.ds(ROWS - EDGE, EDGE)
        main, upper, lower = pl.ds(0, ROWS), pl.ds(ROWS, EDGE), pl.ds(ROWS + EDGE, EDGE)
        right, left = pack_right.at[s, c], pack_left.at[s, c]
        parts = [
            (cur.at[s, c, :, last], top_recv.at[s, c], around[2]),
            (cur.at[s, c, :, first], bot_recv.at[s, c], around[3]),
            (right, left_recv.at[s, c, main], around[0]),
            (left, right_recv.at[s, c, main], around[1]),
            (pack_right.at[s, c, last], left_recv.at[s, c, upper], around[4]),
            (pack_right.at[s, c, first], left_recv.at[s, c, lower], around[5]),
            (pack_left.at[s, c, last], right_recv.at[s, c, upper], around[6]),
            (pack_left.at[s, c, first], right_recv.at[s, c, lower], around[7]),
        ]
        return [
            remote(src, dst, send_sem.at[s, c, n], recv_sem.at[s, c, n], place)
            for n, (src, dst, place) in enumerate(parts)
        ]

    top = offsets_ref[0, 0, 0]
    left = offsets_ref[0, 0, 1]
    info_send[0:8] = jnp.full((8, LANES), top.astype(F32), F32)
    info_send[8:16] = jnp.full((8, LANES), left.astype(F32), F32)
    for copy in info_copies():
        copy.start()

    def one_hot(cond):
        return jnp.where(cond, 1.0, 0.0).astype(BF16)

    half = COLS // 2
    shift_a = one_hot(_iota((half, half), 1) - _iota((half, half), 0) == left)
    shift_b = one_hot(_iota((384, half), 1) - _iota((384, half), 0) + LANES == left)
    shift_c = one_hot(_iota((160, LANES), 1) - _iota((160, LANES), 0) + LANES == left)
    row, col = _iota((4 * ROWS, 2 * TROWS), 0), _iota((4 * ROWS, 2 * TROWS), 1)
    row_odd = lax.rem(row, 2 * ROWS) >= ROWS
    col_odd = col >= TROWS
    row_at = lax.rem(row, ROWS) + jnp.where(row >= 2 * ROWS, ROWS, 0)
    col_at = col - jnp.where(col_odd, TROWS, 0)
    lower_it = one_hot((row_odd == col_odd) & (row_at - col_at == top))

    def dot(a, b):
        return jnp.dot(a, b, preferred_element_type=F32)

    @pl.loop(0, CH)
    def _(c):
        tile = tiles_ref[c].reshape(NZ * TROWS, TCOLS)
        shifted[:, 0:half] = dot(tile[:, 0:half], shift_a).astype(BF16)
        shifted[:, half:COLS] = dot(tile[:, LANES:COLS], shift_b).astype(BF16)
        shifted[:, COLS:] = dot(tile[:, COLS - LANES :], shift_c).astype(BF16)
        for p in range(NZ // 2):
            placed = dot(lower_it, shifted[2 * p * TROWS : 2 * (p + 1) * TROWS, :])
            for zz in range(2):
                own[c, 2 * p + zz] = placed[zz * ROWS : (zz + 1) * ROWS, :COLS].astype(BF16)
                low_send[c, 2 * p + zz] = placed[(2 + zz) * ROWS : (3 + zz) * ROWS, :COLS].astype(BF16)
            for part in range(2):
                even = placed[2 * part * ROWS : (2 * part + 1) * ROWS, COLS:]
                odd = placed[(2 * part + 1) * ROWS : (2 * part + 2) * ROWS, COLS:]
                side_send[c, part, p] = (even + pltpu.roll(odd, 64, 1)).astype(BF16)
        for copy in join_copies(c):
            copy.start()

    @pl.loop(0, CH)
    def _(c):
        def total(a):
            t = psf_ref[c, a, 0]
            for k in range(1, TAPS):
                t = t + psf_ref[c, a, k]
            return t

        inv_x = 1.0 / jnp.full((1, LANES), total(2), F32)
        inv_zy = 1.0 / jnp.full((1, LANES), total(0) * total(1), F32)

        def banded(axis, diff, ks=range(TAPS)):
            ahead = jnp.zeros(diff.shape, F32)
            back = jnp.zeros(diff.shape, F32)
            for k in ks:
                hit = diff == k
                ahead = jnp.where(hit, psf_ref[c, axis, k], ahead)
                back = jnp.where(hit, psf_ref[c, axis, TAPS - 1 - k], back)
            return ahead, back

        square = (LANES, LANES)
        across = _iota(square, 0) - _iota(square, 1)
        for a, shift in enumerate((-113, 15, 143)):
            for d, block in enumerate(banded(2, across + shift)):
                block = (block * inv_x).astype(BF16)
                mat_x[d, c, a * LANES : (a + 1) * LANES, 0:LANES] = block
                mat_x[d, c, (a + 1) * LANES : (a + 2) * LANES, LANES:] = block
        zero = jnp.zeros(square, BF16)
        for d in range(2):
            mat_x[d, c, 0:LANES, LANES:] = zero
            mat_x[d, c, 3 * LANES :, 0:LANES] = zero

        yo = _iota((ROWS, LANES), 0)
        lane = _iota((ROWS, LANES), 1)
        inner = banded(1, lax.rem(lane, ROWS) - yo + HALF)
        above = banded(1, lax.rem(lane, EDGE) - EDGE - yo + HALF)
        below = banded(1, lax.rem(lane, EDGE) + ROWS - yo + HALF)
        has_above = jnp.where(gy > 0, 1.0, 0.0).astype(F32)
        has_below = jnp.where(gy < n_gy - 1, 1.0, 0.0).astype(F32)
        zo = _iota((NZ, LANES), 0)
        zlane = _iota((NZ, LANES), 1)
        depth_taps = range(HALF - NZ + 1, HALF + NZ)
        depth_own = [
            banded(0, 2 * j + lax.div(zlane, ROWS) - zo + HALF, depth_taps) for j in range(4)
        ]
        depth_edge = banded(0, lax.div(zlane, EDGE) - zo + HALF, depth_taps)
        for d in range(2):
            y_own = inner[d] * inv_zy
            y_above = above[d] * inv_zy * has_above
            y_below = below[d] * inv_zy * has_below
            for z in range(NZ):
                at_rows = slice(z * ROWS, (z + 1) * ROWS)
                for j in range(4):
                    mat_zy[d, c, at_rows, j * LANES : (j + 1) * LANES] = (
                        y_own * depth_own[j][d][z : z + 1]
                    ).astype(BF16)
                mat_zy[d, c, at_rows, 4 * LANES : 5 * LANES] = (
                    y_above * depth_edge[d][z : z + 1]
                ).astype(BF16)
                mat_zy[d, c, at_rows, 5 * LANES :] = (y_below * depth_edge[d][z : z + 1]).astype(BF16)

    for copy in info_copies():
        copy.wait_recv()
    has_west = jnp.where(gx > 0, 1.0, 0.0).astype(F32)
    has_north = jnp.where(gy > 0, 1.0, 0.0).astype(F32)
    r = _iota((ROWS, COLS), 0).astype(F32)
    x = _iota((ROWS, COLS), 1).astype(F32)

    def told(n):
        t = jnp.broadcast_to(info_recv[n, 0:1, 0:1], (ROWS, COLS))
        l = jnp.broadcast_to(info_recv[n, 8:9, 0:1], (ROWS, COLS))
        return t, l

    def covers(cond):
        return jnp.where(cond, 1.0, 0.0)

    count = covers((r >= top.astype(F32)) & (x >= left.astype(F32)))
    t, l = told(0)
    count = count + has_west * covers((r >= t) & (x < l + float(MARGIN)))
    t, l = told(1)
    count = count + has_north * covers((r < t + float(MARGIN)) & (x >= l))
    t, l = told(2)
    count = count + has_west * has_north * covers((r < t + float(MARGIN)) & (x < l + float(MARGIN)))
    recip[...] = 1.0 / count

    lane = _iota((ROWS, LANES), 1)

    def pack_edges(s, c, plane):
        right = jnp.zeros((ROWS, LANES), F32)
        left_side = jnp.zeros((ROWS, LANES), F32)
        for z in range(NZ):
            here = lax.div(lane, EDGE) == z
            field = plane(z)
            right = jnp.where(
                here, pltpu.roll(field[:, COLS - LANES :], (EDGE * z + EDGE) % LANES, 1), right
            )
            left_side = jnp.where(here, pltpu.roll(field[:, :LANES], EDGE * z, 1), left_side)
        pack_right[s, c] = right.astype(BF16)
        pack_left[s, c] = left_side.astype(BF16)

    @pl.loop(0, CH)
    def _(c):
        for copy in join_copies(c):
            copy.wait_recv()
        for z in range(NZ):
            total = own[c, z].astype(F32) + has_north * low_recv[c, z].astype(F32)
            spill = has_west * (
                side_recv[c, 0, z // 2].astype(F32) + has_north * side_recv[c, 1, z // 2].astype(F32)
            )
            if z % 2:
                spill = pltpu.roll(spill, 64, 1)
            spill = jnp.where(lane < 64, spill, 0.0)
            total = jnp.concatenate([total[:, :LANES] + spill, total[:, LANES:]], axis=1)
            value = total * recip[...]
            joined[c, z] = value
            est_ref[c, z] = value
            cur[0, c, z] = value.astype(BF16)
        pack_edges(0, c, lambda z: joined[c, z])
        for copy in halo_copies(0, c):
            copy.start()

    wide_lane = _iota((ROWS + 2 * EDGE, LANES), 1)
    from_west = (wide_lane >= LANES - EDGE) & (gx > 0)
    from_east = (wide_lane < EDGE) & (gx < n_gx - 1)

    def unpack_edges(s, c):
        west_side = left_recv[s, c].astype(F32)
        east_side = right_recv[s, c].astype(F32)
        for z in range(NZ):
            tile = jnp.where(
                from_west,
                pltpu.roll(west_side, (2 * LANES - EDGE - EDGE * z) % LANES, 1),
                jnp.where(from_east, pltpu.roll(east_side, (LANES - EDGE * z) % LANES, 1), 0.0),
            ).astype(BF16)
            edge[z * ROWS : (z + 1) * ROWS] = tile[:ROWS]
            edge[OWN + z * EDGE : OWN + (z + 1) * EDGE] = tile[ROWS : ROWS + EDGE]
            edge[OWN + STRIP + z * EDGE : OWN + STRIP + (z + 1) * EDGE] = tile[ROWS + EDGE :]

    def segments(s, c):
        return (
            (0, OWN, cur[s, c].reshape(OWN, COLS)),
            (OWN, STRIP, top_recv[s, c].reshape(STRIP, COLS)),
            (OWN + STRIP, STRIP, bot_recv[s, c].reshape(STRIP, COLS)),
        )

    def blur(d, s, c):
        unpack_edges(s, c)
        taps = mat_x[d, c]
        for start, size, field in segments(s, c):
            side = edge[start : start + size]
            first = jnp.concatenate([side, field[:, : COLS - LANES]], axis=1)
            spread[start : start + size, :half] = dot(first, taps).astype(BF16)
            second = jnp.concatenate([field[:, LANES:], side], axis=1)
            spread[start : start + size, half:] = dot(second, taps).astype(BF16)

    @pl.loop(0, ITERS)
    def _(it):
        for d in range(2):
            s = 2 * it + d

            @pl.loop(0, CH)
            def _(c):
                for copy in halo_copies(s, c):
                    copy.wait_recv()
                blur(d, s, c)
                for z in range(0, NZ, 2):
                    seen = dot(mat_zy[d, c, z * ROWS : (z + 2) * ROWS], spread[...])
                    seen = seen.reshape(2, ROWS, COLS)
                    if d == 0:
                        value = joined[c, z : z + 2] / seen
                    else:
                        value = est_ref[c, z : z + 2] * seen
                        est_ref[c, z : z + 2] = value
                    cur[s + 1, c, z : z + 2] = value.astype(BF16)
                pack_edges(s + 1, c, lambda z: cur[s + 1, c, z].astype(F32))
                for copy in halo_copies(s + 1, c):
                    copy.start()

    rows_of = jnp.where(gy == 0, prow_ref[1], jnp.where(gy == n_gy - 1, prow_ref[2], prow_ref[0]))
    cols_of = jnp.where(gx == 0, ptwo_ref[1], jnp.where(gx == n_gx - 1, ptwo_ref[2], ptwo_ref[0]))
    n_one = NZ * ROWS // 4
    last = STEPS - 1

    @pl.loop(0, CH)
    def _(c):
        for copy in halo_copies(last, c):
            copy.wait_recv()
        unpack_edges(last, c)
        main = jnp.zeros((rows_of.shape[0], COLS), F32)
        for start, size, field in segments(last, c):
            main = main + dot(rows_of[:, start : start + size], field)
        side = dot(rows_of, edge[...])
        tall = jnp.concatenate([side, main], axis=1).astype(BF16)
        one = dot(tall[:n_one], pone_ref[...])
        one_ref[c] = one.reshape(NZ // 2, ROWS // 2, COLS // 2)
        two = dot(tall[n_one:], cols_of)
        two_ref[c] = two.reshape(NZ // 4, ROWS // 4, COLS // 4)

    for copy in info_copies():
        copy.wait_send()

    @pl.loop(0, CH)
    def _(c):
        for copy in join_copies(c):
            copy.wait_send()

        @pl.loop(0, STEPS)
        def _(s):
            for copy in halo_copies(s, c):
                copy.wait_send()


def solution(mesh):
    import functools

    sizes = (mesh.shape["gx"], mesh.shape["gy"])
    prow = _pyramid_rows()
    pone, ptwo = _pyramid_cols()
    smem = pl.BlockSpec(memory_space=pltpu.SMEM)
    vmem = pl.BlockSpec(memory_space=pltpu.VMEM)
    dma = pltpu.SemaphoreType.DMA

    def per_device(tiles, offsets, psf):
        return pl.pallas_call(
            functools.partial(_kernel, sizes),
            out_shape=(
                jax.ShapeDtypeStruct((CH, NZ, ROWS, COLS), F32),
                jax.ShapeDtypeStruct((CH, NZ // 2, ROWS // 2, COLS // 2), F32),
                jax.ShapeDtypeStruct((CH, NZ // 4, ROWS // 4, COLS // 4), F32),
            ),
            in_specs=[smem, smem, vmem, vmem, vmem, vmem],
            out_specs=(vmem, vmem, vmem),
            scratch_shapes=[
                pltpu.VMEM((NZ * TROWS, COLS + LANES), BF16),
                pltpu.VMEM((CH, NZ, ROWS, COLS), BF16),
                pltpu.VMEM((CH, NZ, ROWS, COLS), BF16),
                pltpu.VMEM((CH, NZ, ROWS, COLS), BF16),
                pltpu.VMEM((CH, 2, NZ // 2, ROWS, LANES), BF16),
                pltpu.VMEM((CH, 2, NZ // 2, ROWS, LANES), BF16),
                pltpu.VMEM((16, LANES), F32),
                pltpu.VMEM((3, 16, LANES), F32),
                pltpu.VMEM((ROWS, COLS), F32),
                pltpu.VMEM((CH, NZ, ROWS, COLS), F32),
                pltpu.VMEM((STEPS, CH, NZ, ROWS, COLS), BF16),
                pltpu.VMEM((STEPS, CH, NZ, EDGE, COLS), BF16),
                pltpu.VMEM((STEPS, CH, NZ, EDGE, COLS), BF16),
                pltpu.VMEM((STEPS, CH, ROWS, LANES), BF16),
                pltpu.VMEM((STEPS, CH, ROWS, LANES), BF16),
                pltpu.VMEM((STEPS, CH, ROWS + 2 * EDGE, LANES), BF16),
                pltpu.VMEM((STEPS, CH, ROWS + 2 * EDGE, LANES), BF16),
                pltpu.VMEM((ALL, LANES), BF16),
                pltpu.VMEM((ALL, COLS), BF16),
                pltpu.VMEM((2, CH, COLS, COLS // 2), BF16),
                pltpu.VMEM((2, CH, OWN, ALL), BF16),
                dma((CH, 3)),
                dma((CH, 3)),
                dma((3,)),
                dma((3,)),
                dma((STEPS, CH, 8)),
                dma((STEPS, CH, 8)),
            ],
            compiler_params=pltpu.CompilerParams(
                collective_id=0, has_side_effects=True, vmem_limit_bytes=60 * 1024 * 1024
            ),
        )(offsets, psf, tiles, jnp.asarray(prow), jnp.asarray(pone), jnp.asarray(ptwo))

    in_specs = (P(None, None, "gy", "gx"), P("gy", "gx", None), P())
    out_specs = (P(None, None, "gy", "gx"),) * 3
    return jax.shard_map(
        per_device, mesh=mesh, in_specs=in_specs, out_specs=out_specs, check_vma=False
    )
```

profile of v0, /device:TPU:1, one launch (start us, length us, event | category | flops | bytes accessed | tf_op | source)
XLA Modules:
  0.0 74.5 jit_solution(12109597192743634764)
XLA Ops:
  0.6 68.4 %shard_map.85 = (f32[3,8,64,512]{3,2,1,0:T(8,128)}, f32[3,4,32,256]{3,2,1,0:T(8,128)}, f32[3,2,16,128]{3,2,1,0:T(8,128)}) custom-call(s32[1,1,2]{2,1,0:T(1,128)} %offsets_ref.1, f32[3,3,31]{2,1,0:T(4,128)} %psf_ref.1, bf16[3,8,96,544]{3,2,1,0:T(8,128)(2,1)} %tiles_ref.1, bf16[3,160,768]{2,1,0:T(8,128)(2,1)} %constant.6.clone.prow_ref, ...), custom_call_target="tpu_custom_call" | custom-call | tf_op jit(solution)/shard_map/pallas_call | solution.py:446
  69.0 0.0 copy-start
  69.0 0.0 copy-start.1
  69.0 4.1 %copy.12 = f32[3,8,64,512]{3,2,1,0:T(8,128)} copy(f32[3,8,64,512]{3,2,1,0:T(8,128)} %get-tuple-element.6) | data formatting | bytes 6291456
  73.1 0.0 copy-done
  73.1 0.7 %copy.13 = f32[3,4,32,256]{3,2,1,0:T(8,128)} copy(f32[3,4,32,256]{3,2,1,0:T(8,128)S(1)} %copy-done) | data formatting | bytes 786432
  73.8 0.0 copy-done.1
  73.8 0.6 copy.14
Async XLA Ops:
  69.0 4.1 %copy-start = (f32[3,4,32,256]{3,2,1,0:T(8,128)S(1)}, f32[3,4,32,256]{3,2,1,0:T(8,128)}, u32[]{:S(2)}) copy-start(f32[3,4,32,256]{3,2,1,0:T(8,128)} %get-tuple-element.7) | copy-start | bytes 1179652
  69.0 4.8 %copy-start.1 = (f32[3,2,16,128]{3,2,1,0:T(8,128)S(1)}, f32[3,2,16,128]{3,2,1,0:T(8,128)}, u32[]{:S(2)}) copy-start(f32[3,2,16,128]{3,2,1,0:T(8,128)} %get-tuple-element.8) | copy-start | bytes 147460
where the time goes:
time: 74.6 us; the launch traced here: 74.5 us
  Pallas kernels  68.4 us (92%)
  local copies, waits for them, and re-layouts  5.45 us (7%)
    pallas_call x1, Pallas kernels, per_device(): pl.pallas_call(functools.partial(_kernel, sizes), out_shape=(jax.ShapeDty...  68.4 us
    unnamed x7, local copies, waits for them, and re-layouts  5.45 us

commit v1 on v0

--- a/solution.py
+++ b/solution.py
@@ -1,3 +1,5 @@
+import functools
+
 import jax
 import jax.numpy as jnp
 import numpy as np
@@ -20,6 +22,7 @@
 LANES = 128
 OWN, STRIP = NZ * ROWS, NZ * EDGE
 ALL = OWN + 2 * STRIP
+GROUP = 4
 
 GAUSS = np.array([1.0, 4.0, 6.0, 4.0, 1.0]) / 16.0
 
@@ -90,6 +93,10 @@
     est_ref,
     one_ref,
     two_ref,
+    tiles_in,
+    prow_in,
+    pone_in,
+    ptwo_in,
     shifted,
     own,
     low_send,
@@ -101,8 +108,7 @@
     recip,
     joined,
     cur,
-    top_recv,
-    bot_recv,
+    strip_recv,
     pack_right,
     pack_left,
     left_recv,
@@ -111,6 +117,7 @@
     spread,
     mat_x,
     mat_zy,
+    load_sem,
     join_send_sem,
     join_recv_sem,
     info_send_sem,
@@ -139,7 +146,18 @@
     barrier = pltpu.get_barrier_semaphore()
     for place in around:
         pl.semaphore_signal(barrier, inc=1, device_id=place, device_id_type=MESH)
-    pl.semaphore_wait(barrier, len(around))
+
+    tile_loads = [
+        pltpu.make_async_copy(tiles_ref.at[c], tiles_in.at[c], load_sem.at[c]) for c in range(CH)
+    ]
+    constant_loads = [
+        pltpu.make_async_copy(src, dst, load_sem.at[CH + n])
+        for n, (src, dst) in enumerate(
+            ((prow_ref, prow_in), (pone_ref, pone_in), (ptwo_ref, ptwo_in))
+        )
+    ]
+    for copy in tile_loads + constant_loads:
+        copy.start()
 
     def remote(src, dst, send, recv, place):
         return pltpu.make_async_remote_copy(
@@ -159,13 +177,28 @@
             for n, k in enumerate((0, 2, 4))
         ]
 
-    def halo_copies(s, c):
-        first, last = pl.ds(0, EDGE), pl.ds(ROWS - EDGE, EDGE)
-        main, upper, lower = pl.ds(0, ROWS), pl.ds(ROWS, EDGE), pl.ds(ROWS + EDGE, EDGE)
+    def row_copies(s, c, planes=slice(0, NZ), rows=EDGE):
+        z = pl.ds(planes.start, planes.stop - planes.start)
+        parts = [
+            (pl.ds(ROWS - rows, rows), 0, pl.ds(EDGE - rows, rows), around[2]),
+            (pl.ds(0, rows), 1, pl.ds(0, rows), around[3]),
+        ]
+        return [
+            remote(
+                cur.at[s, c, z, src],
+                strip_recv.at[s, c, n, z, dst],
+                send_sem.at[s, c, n],
+                recv_sem.at[s, c, n],
+                place,
+            )
+            for src, n, dst, place in parts
+        ]
+
+    def edge_copies(s, c, rows=EDGE):
+        first, last, main = pl.ds(0, rows), pl.ds(ROWS - rows, rows), pl.ds(0, ROWS)
+        upper, lower = pl.ds(ROWS + EDGE - rows, rows), pl.ds(ROWS + EDGE, rows)
         right, left = pack_right.at[s, c], pack_left.at[s, c]
         parts = [
-            (cur.at[s, c, :, last], top_recv.at[s, c], around[2]),
-            (cur.at[s, c, :, first], bot_recv.at[s, c], around[3]),
             (right, left_recv.at[s, c, main], around[0]),
             (left, right_recv.at[s, c, main], around[1]),
             (pack_right.at[s, c, last], left_recv.at[s, c, upper], around[4]),
@@ -174,16 +207,18 @@
             (pack_left.at[s, c, first], right_recv.at[s, c, lower], around[7]),
         ]
         return [
-            remote(src, dst, send_sem.at[s, c, n], recv_sem.at[s, c, n], place)
+            remote(src, dst, send_sem.at[s, c, 2 + n], recv_sem.at[s, c, 2 + n], place)
             for n, (src, dst, place) in enumerate(parts)
         ]
+
+    def start(copies):
+        for copy in copies:
+            copy.start()
 
     top = offsets_ref[0, 0, 0]
     left = offsets_ref[0, 0, 1]
     info_send[0:8] = jnp.full((8, LANES), top.astype(F32), F32)
     info_send[8:16] = jnp.full((8, LANES), left.astype(F32), F32)
-    for copy in info_copies():
-        copy.start()
 
     def one_hot(cond):
         return jnp.where(cond, 1.0, 0.0).astype(BF16)
@@ -202,9 +237,21 @@
     def dot(a, b):
         return jnp.dot(a, b, preferred_element_type=F32)
 
+    unused = jnp.zeros((CH, NZ, EDGE // 2, COLS), BF16)
+    strip_recv[STEPS - 1, :, 0, :, : EDGE // 2] = unused
+    strip_recv[STEPS - 1, :, 1, :, EDGE // 2 :] = unused
+    unused = jnp.zeros((CH, EDGE // 2, LANES), BF16)
+    for side_recv_ref in (left_recv, right_recv):
+        side_recv_ref[STEPS - 1, :, ROWS : ROWS + EDGE // 2] = unused
+        side_recv_ref[STEPS - 1, :, ROWS + EDGE + EDGE // 2 :] = unused
+
+    pl.semaphore_wait(barrier, len(around))
+    start(info_copies())
+
     @pl.loop(0, CH)
     def _(c):
-        tile = tiles_ref[c].reshape(NZ * TROWS, TCOLS)
+        pltpu.make_async_copy(tiles_ref.at[c], tiles_in.at[c], load_sem.at[c]).wait()
+        tile = tiles_in[c].reshape(NZ * TROWS, TCOLS)
         shifted[:, 0:half] = dot(tile[:, 0:half], shift_a).astype(BF16)
         shifted[:, half:COLS] = dot(tile[:, LANES:COLS], shift_b).astype(BF16)
         shifted[:, COLS:] = dot(tile[:, COLS - LANES :], shift_c).astype(BF16)
@@ -217,8 +264,7 @@
                 even = placed[2 * part * ROWS : (2 * part + 1) * ROWS, COLS:]
                 odd = placed[(2 * part + 1) * ROWS : (2 * part + 2) * ROWS, COLS:]
                 side_send[c, part, p] = (even + pltpu.roll(odd, 64, 1)).astype(BF16)
-        for copy in join_copies(c):
-            copy.start()
+        start(join_copies(c))
 
     @pl.loop(0, CH)
     def _(c):
@@ -337,9 +383,9 @@
             joined[c, z] = value
             est_ref[c, z] = value
             cur[0, c, z] = value.astype(BF16)
+        start(row_copies(0, c))
         pack_edges(0, c, lambda z: joined[c, z])
-        for copy in halo_copies(0, c):
-            copy.start()
+        start(edge_copies(0, c))
 
     wide_lane = _iota((ROWS + 2 * EDGE, LANES), 1)
     from_west = (wide_lane >= LANES - EDGE) & (gx > 0)
@@ -361,61 +407,73 @@
     def segments(s, c):
         return (
             (0, OWN, cur[s, c].reshape(OWN, COLS)),
-            (OWN, STRIP, top_recv[s, c].reshape(STRIP, COLS)),
-            (OWN + STRIP, STRIP, bot_recv[s, c].reshape(STRIP, COLS)),
+            (OWN, 2 * STRIP, strip_recv[s, c].reshape(2 * STRIP, COLS)),
         )
 
     def blur(d, s, c):
         unpack_edges(s, c)
         taps = mat_x[d, c]
-        for start, size, field in segments(s, c):
-            side = edge[start : start + size]
+        for begin, size, field in segments(s, c):
+            side = edge[begin : begin + size]
             first = jnp.concatenate([side, field[:, : COLS - LANES]], axis=1)
-            spread[start : start + size, :half] = dot(first, taps).astype(BF16)
+            spread[begin : begin + size, :half] = dot(first, taps).astype(BF16)
             second = jnp.concatenate([field[:, LANES:], side], axis=1)
-            spread[start : start + size, half:] = dot(second, taps).astype(BF16)
-
-    @pl.loop(0, ITERS)
+            spread[begin : begin + size, half:] = dot(second, taps).astype(BF16)
+
+    last = STEPS - 1
+
+    def iterate(it, d, final):
+        s = 2 * it + d
+        rows = EDGE // 2 if final else EDGE
+
+        @pl.loop(0, CH)
+        def _(c):
+            for copy in row_copies(s, c) + edge_copies(s, c):
+                copy.wait_recv()
+            blur(d, s, c)
+            for z in range(0, NZ, GROUP):
+                planes = slice(z, z + GROUP)
+                seen = dot(mat_zy[d, c, z * ROWS : (z + GROUP) * ROWS], spread[...])
+                seen = seen.reshape(GROUP, ROWS, COLS)
+                if d == 0:
+                    value = joined[c, planes] / seen
+                else:
+                    value = est_ref[c, planes] * seen
+                    est_ref[c, planes] = value
+                cur[s + 1, c, planes] = value.astype(BF16)
+                start(row_copies(s + 1, c, planes, rows))
+            pack_edges(s + 1, c, lambda z: cur[s + 1, c, z].astype(F32))
+            start(edge_copies(s + 1, c, rows))
+
+    @pl.loop(0, ITERS - 1)
     def _(it):
-        for d in range(2):
-            s = 2 * it + d
-
-            @pl.loop(0, CH)
-            def _(c):
-                for copy in halo_copies(s, c):
-                    copy.wait_recv()
-                blur(d, s, c)
-                for z in range(0, NZ, 2):
-                    seen = dot(mat_zy[d, c, z * ROWS : (z + 2) * ROWS], spread[...])
-                    seen = seen.reshape(2, ROWS, COLS)
-                    if d == 0:
-                        value = joined[c, z : z + 2] / seen
-                    else:
-                        value = est_ref[c, z : z + 2] * seen
-                        est_ref[c, z : z + 2] = value
-                    cur[s + 1, c, z : z + 2] = value.astype(BF16)
-                pack_edges(s + 1, c, lambda z: cur[s + 1, c, z].astype(F32))
-                for copy in halo_copies(s + 1, c):
-                    copy.start()
-
-    rows_of = jnp.where(gy == 0, prow_ref[1], jnp.where(gy == n_gy - 1, prow_ref[2], prow_ref[0]))
-    cols_of = jnp.where(gx == 0, ptwo_ref[1], jnp.where(gx == n_gx - 1, ptwo_ref[2], ptwo_ref[0]))
+        iterate(it, 0, False)
+        iterate(it, 1, False)
+
+    iterate(ITERS - 1, 0, False)
+    iterate(ITERS - 1, 1, True)
+
+    for copy in constant_loads:
+        copy.wait()
+    rows_of = jnp.where(gy == 0, prow_in[1], jnp.where(gy == n_gy - 1, prow_in[2], prow_in[0]))
+    cols_of = jnp.where(gx == 0, ptwo_in[1], jnp.where(gx == n_gx - 1, ptwo_in[2], ptwo_in[0]))
     n_one = NZ * ROWS // 4
-    last = STEPS - 1
 
     @pl.loop(0, CH)
     def _(c):
-        for copy in halo_copies(last, c):
+        for copy in row_copies(last, c, rows=EDGE // 2) + edge_copies(last, c, EDGE // 2):
             copy.wait_recv()
         unpack_edges(last, c)
         main = jnp.zeros((rows_of.shape[0], COLS), F32)
-        for start, size, field in segments(last, c):
-            main = main + dot(rows_of[:, start : start + size], field)
+        for begin, size, field in segments(last, c):
+            main = main + dot(rows_of[:, begin : begin + size], field)
         side = dot(rows_of, edge[...])
-        tall = jnp.concatenate([side, main], axis=1).astype(BF16)
-        one = dot(tall[:n_one], pone_ref[...])
+        tall = jnp.concatenate([side, main], axis=1)
+        high = tall.astype(BF16)
+        low = (tall - high.astype(F32)).astype(BF16)
+        one = dot(high[:n_one], pone_in[...]) + dot(low[:n_one], pone_in[...])
         one_ref[c] = one.reshape(NZ // 2, ROWS // 2, COLS // 2)
-        two = dot(tall[n_one:], cols_of)
+        two = dot(high[n_one:], cols_of) + dot(low[n_one:], cols_of)
         two_ref[c] = two.reshape(NZ // 4, ROWS // 4, COLS // 4)
 
     for copy in info_copies():
@@ -426,33 +484,49 @@
         for copy in join_copies(c):
             copy.wait_send()
 
-        @pl.loop(0, STEPS)
+        @pl.loop(0, last)
         def _(s):
-            for copy in halo_copies(s, c):
+            for copy in row_copies(s, c) + edge_copies(s, c):
                 copy.wait_send()
 
+        for copy in row_copies(last, c, rows=EDGE // 2) + edge_copies(last, c, EDGE // 2):
+            copy.wait_send()
+
+
+def _settle(*refs):
+    sem = refs[-1]
+    copies = [pltpu.make_async_copy(refs[n], refs[n + 3], sem.at[n]) for n in range(3)]
+    for copy in copies:
+        copy.start()
+    for copy in copies:
+        copy.wait()
+
 
 def solution(mesh):
-    import functools
 
     sizes = (mesh.shape["gx"], mesh.shape["gy"])
     prow = _pyramid_rows()
     pone, ptwo = _pyramid_cols()
     smem = pl.BlockSpec(memory_space=pltpu.SMEM)
     vmem = pl.BlockSpec(memory_space=pltpu.VMEM)
+    hbm = pl.BlockSpec(memory_space=pltpu.HBM)
     dma = pltpu.SemaphoreType.DMA
 
     def per_device(tiles, offsets, psf):
-        return pl.pallas_call(
+        outs = pl.pallas_call(
             functools.partial(_kernel, sizes),
             out_shape=(
-                jax.ShapeDtypeStruct((CH, NZ, ROWS, COLS), F32),
-                jax.ShapeDtypeStruct((CH, NZ // 2, ROWS // 2, COLS // 2), F32),
-                jax.ShapeDtypeStruct((CH, NZ // 4, ROWS // 4, COLS // 4), F32),
+                pltpu.VMEM((CH, NZ, ROWS, COLS), F32),
+                pltpu.VMEM((CH, NZ // 2, ROWS // 2, COLS // 2), F32),
+                pltpu.VMEM((CH, NZ // 4, ROWS // 4, COLS // 4), F32),
             ),
-            in_specs=[smem, smem, vmem, vmem, vmem, vmem],
+            in_specs=[smem, smem, hbm, hbm, hbm, hbm],
             out_specs=(vmem, vmem, vmem),
             scratch_shapes=[
+                pltpu.VMEM((CH, NZ, TROWS, TCOLS), BF16),
+                pltpu.VMEM(prow.shape, BF16),
+                pltpu.VMEM(pone.shape, BF16),
+                pltpu.VMEM(ptwo.shape, BF16),
                 pltpu.VMEM((NZ * TROWS, COLS + LANES), BF16),
                 pltpu.VMEM((CH, NZ, ROWS, COLS), BF16),
                 pltpu.VMEM((CH, NZ, ROWS, COLS), BF16),
@@ -464,8 +538,7 @@
                 pltpu.VMEM((ROWS, COLS), F32),
                 pltpu.VMEM((CH, NZ, ROWS, COLS), F32),
                 pltpu.VMEM((STEPS, CH, NZ, ROWS, COLS), BF16),
-                pltpu.VMEM((STEPS, CH, NZ, EDGE, COLS), BF16),
-                pltpu.VMEM((STEPS, CH, NZ, EDGE, COLS), BF16),
+                pltpu.VMEM((STEPS, CH, 2, NZ, EDGE, COLS), BF16),
                 pltpu.VMEM((STEPS, CH, ROWS, LANES), BF16),
                 pltpu.VMEM((STEPS, CH, ROWS, LANES), BF16),
                 pltpu.VMEM((STEPS, CH, ROWS + 2 * EDGE, LANES), BF16),
@@ -474,6 +547,7 @@
                 pltpu.VMEM((ALL, COLS), BF16),
                 pltpu.VMEM((2, CH, COLS, COLS // 2), BF16),
                 pltpu.VMEM((2, CH, OWN, ALL), BF16),
+                dma((CH + 3,)),
                 dma((CH, 3)),
                 dma((CH, 3)),
                 dma((3,)),
@@ -482,9 +556,20 @@
                 dma((STEPS, CH, 8)),
             ],
             compiler_params=pltpu.CompilerParams(
-                collective_id=0, has_side_effects=True, vmem_limit_bytes=60 * 1024 * 1024
+                collective_id=0, has_side_effects=True, vmem_limit_bytes=48 * 1024 * 1024
             ),
-        )(offsets, psf, tiles, jnp.asarray(prow), jnp.asarray(pone), jnp.asarray(ptwo))
+        )(*[
+            pltpu.with_memory_space_constraint(x, pltpu.HBM)
+            for x in (offsets, psf, tiles, jnp.asarray(prow), jnp.asarray(pone), jnp.asarray(ptwo))
+        ])
+        return pl.pallas_call(
+            _settle,
+            out_shape=tuple(jax.ShapeDtypeStruct(o.shape, o.dtype) for o in outs),
+            in_specs=[vmem] * 3,
+            out_specs=(hbm,) * 3,
+            scratch_shapes=[dma((3,))],
+            compiler_params=pltpu.CompilerParams(vmem_limit_bytes=4 * 1024 * 1024),
+        )(*[pltpu.with_memory_space_constraint(o, pltpu.VMEM) for o in outs])
 
     in_specs = (P(None, None, "gy", "gx"), P("gy", "gx", None), P())
     out_specs = (P(None, None, "gy", "gx"),) * 3

time: 74.6 us -> 68.2 us (0.914)
  local copies, waits for them, and re-layouts: 5.45 us -> 0 us
  Pallas kernels: 68.4 us -> 67.4 us
    unnamed x7 -> x0, local copies, waits for them, and re-layouts: 5.45 us -> none
    pallas_call x1 -> x2, Pallas kernels: 68.4 us -> 67.4 us  [the longest x1 65.6 us: per_device(): pl.pallas_call(functools.partial(_kernel, sizes), out_shape=(pltpu.VMEM((...]
where the time goes in v1:
time: 68.2 us; the launch traced here: 68.1 us
  Pallas kernels  67.4 us (99%)
    pallas_call x1, Pallas kernels, per_device(): pl.pallas_call(functools.partial(_kernel, sizes), out_shape=(pltpu.VMEM((...  65.6 us
    pallas_call x1, Pallas kernels, per_device(): pl.pallas_call(_settle, out_shape=tuple((jax.ShapeDtypeStruct(o.shape, o....  1.81 us

profile of v1, /device:TPU:1, one launch (start us, length us, event | category | flops | bytes accessed | tf_op | source)
XLA Modules:
  0.0 68.1 jit_solution(11420662304932779157)
XLA Ops:
  0.6 65.6 %shard_map.85 = (f32[3,8,64,512]{3,2,1,0:T(8,128)S(1)}, f32[3,4,32,256]{3,2,1,0:T(8,128)S(1)}, f32[3,2,16,128]{3,2,1,0:T(8,128)S(1)}) custom-call(s32[1,1,2]{2,1,0:T(1,128)} %offsets_ref.1, f32[3,3,31]{2,1,0:T(4,128)} %psf_ref.1, bf16[3,8,96,544]{3,2,1,0:T(8,128)(2,1)} %tiles_ref.1, bf16[3,160,768]{2,1,0:T(8,128)(2,1)} %constant.6.clone.prow_ref, ...), custom_call_target="tpu_custom_call" | custom-call | tf_op jit(solution)/shard_map/pallas_call | solution.py:516
  66.3 1.8 %shard_map.86 = (f32[3,8,64,512]{3,2,1,0:T(8,128)}, f32[3,4,32,256]{3,2,1,0:T(8,128)}, f32[3,2,16,128]{3,2,1,0:T(8,128)}) custom-call(f32[3,8,64,512]{3,2,1,0:T(8,128)S(1)} %get-tuple-element.6.refs_0_, f32[3,4,32,256]{3,2,1,0:T(8,128)S(1)} %get-tuple-element.7.refs_1_, f32[3,2,16,128]{3,2,1,0:T(8,128)S(1)} %get-tuple-element.8.refs_2_), custom_call_target="tpu_custom_call" | custom-call | tf_op jit(solution)/shard_map/pallas_call | solution.py:565

commit v2 on v1

--- a/solution.py
+++ b/solution.py
@@ -19,10 +19,10 @@
 ITERS = 2
 STEPS = 2 * ITERS + 1
 EDGE = 16
+RELAY = 2
 LANES = 128
 OWN, STRIP = NZ * ROWS, NZ * EDGE
 ALL = OWN + 2 * STRIP
-GROUP = 4
 
 GAUSS = np.array([1.0, 4.0, 6.0, 4.0, 1.0]) / 16.0
 
@@ -84,8 +84,8 @@
 
 def _kernel(
     sizes,
-    offsets_ref,
-    psf_ref,
+    offsets_in,
+    psf_in,
     tiles_ref,
     prow_ref,
     pone_ref,
@@ -93,6 +93,8 @@
     est_ref,
     one_ref,
     two_ref,
+    offsets_ref,
+    psf_ref,
     tiles_in,
     prow_in,
     pone_in,
@@ -120,6 +122,9 @@
     load_sem,
     join_send_sem,
     join_recv_sem,
+    relay,
+    relay_send_sem,
+    relay_recv_sem,
     info_send_sem,
     info_recv_sem,
     send_sem,
@@ -143,8 +148,10 @@
         at(west, south),
         at(west, north),
     ]
+    odd = lax.rem(gy, 2) == 1
+    ring = [at(gx, lax.rem(gy + k, n_gy)) for k in (n_gy - 2, n_gy - 3, 2, 3)]
     barrier = pltpu.get_barrier_semaphore()
-    for place in around:
+    for place in around + ring:
         pl.semaphore_signal(barrier, inc=1, device_id=place, device_id_type=MESH)
 
     tile_loads = [
@@ -156,7 +163,9 @@
             ((prow_ref, prow_in), (pone_ref, pone_in), (ptwo_ref, ptwo_in))
         )
     ]
-    for copy in tile_loads + constant_loads:
+    offsets_load = pltpu.make_async_copy(offsets_in, offsets_ref, load_sem.at[CH + 3])
+    psf_load = pltpu.make_async_copy(psf_in, psf_ref, load_sem.at[CH + 4])
+    for copy in [offsets_load, *tile_loads, psf_load, *constant_loads]:
         copy.start()
 
     def remote(src, dst, send, recv, place):
@@ -166,10 +175,33 @@
 
     def join_copies(c):
         return [
-            remote(low_send.at[c], low_recv.at[c], join_send_sem.at[c, 0], join_recv_sem.at[c, 0], around[2]),
             remote(side_send.at[c, 0], side_recv.at[c, 0], join_send_sem.at[c, 1], join_recv_sem.at[c, 1], around[0]),
             remote(side_send.at[c, 1], side_recv.at[c, 1], join_send_sem.at[c, 2], join_recv_sem.at[c, 2], around[4]),
         ]
+
+    def lower_copy(c, planes=slice(0, NZ - RELAY)):
+        z = pl.ds(planes.start, planes.stop - planes.start)
+        return remote(
+            low_send.at[c, z], low_recv.at[c, z], join_send_sem.at[c, 0], join_recv_sem.at[c, 0], around[2]
+        )
+
+    far = pl.ds(NZ - RELAY, RELAY)
+
+    def far_copy(c):
+        return remote(
+            low_send.at[c, far], low_recv.at[c, far], relay_send_sem.at[c, 0], relay_recv_sem.at[c, 0], around[2]
+        )
+
+    def relay_copy(c, hop):
+        src = low_send.at[c, far] if hop == 0 else relay.at[c, hop - 1]
+        dst = low_recv.at[c, far] if hop == 2 else relay.at[c, hop]
+        return remote(
+            src,
+            dst,
+            relay_send_sem.at[c, hop],
+            relay_recv_sem.at[c, 0 if hop == 2 else hop + 1],
+            ring[1] if hop == 2 else ring[0],
+        )
 
     def info_copies():
         return [
@@ -177,16 +209,15 @@
             for n, k in enumerate((0, 2, 4))
         ]
 
-    def row_copies(s, c, planes=slice(0, NZ), rows=EDGE):
-        z = pl.ds(planes.start, planes.stop - planes.start)
+    def row_copies(s, c, rows=EDGE):
         parts = [
             (pl.ds(ROWS - rows, rows), 0, pl.ds(EDGE - rows, rows), around[2]),
             (pl.ds(0, rows), 1, pl.ds(0, rows), around[3]),
         ]
         return [
             remote(
-                cur.at[s, c, z, src],
-                strip_recv.at[s, c, n, z, dst],
+                cur.at[s, c, :, src],
+                strip_recv.at[s, c, n, :, dst],
                 send_sem.at[s, c, n],
                 recv_sem.at[s, c, n],
                 place,
@@ -215,6 +246,7 @@
         for copy in copies:
             copy.start()
 
+    offsets_load.wait()
     top = offsets_ref[0, 0, 0]
     left = offsets_ref[0, 0, 1]
     info_send[0:8] = jnp.full((8, LANES), top.astype(F32), F32)
@@ -245,7 +277,7 @@
         side_recv_ref[STEPS - 1, :, ROWS : ROWS + EDGE // 2] = unused
         side_recv_ref[STEPS - 1, :, ROWS + EDGE + EDGE // 2 :] = unused
 
-    pl.semaphore_wait(barrier, len(around))
+    pl.semaphore_wait(barrier, len(around) + len(ring))
     start(info_copies())
 
     @pl.loop(0, CH)
@@ -255,16 +287,30 @@
         shifted[:, 0:half] = dot(tile[:, 0:half], shift_a).astype(BF16)
         shifted[:, half:COLS] = dot(tile[:, LANES:COLS], shift_b).astype(BF16)
         shifted[:, COLS:] = dot(tile[:, COLS - LANES :], shift_c).astype(BF16)
-        for p in range(NZ // 2):
+        for p in (NZ // 2 - 1, *range(NZ // 2 - 1)):
             placed = dot(lower_it, shifted[2 * p * TROWS : 2 * (p + 1) * TROWS, :])
             for zz in range(2):
                 own[c, 2 * p + zz] = placed[zz * ROWS : (zz + 1) * ROWS, :COLS].astype(BF16)
                 low_send[c, 2 * p + zz] = placed[(2 + zz) * ROWS : (3 + zz) * ROWS, :COLS].astype(BF16)
             for part in range(2):
                 even = placed[2 * part * ROWS : (2 * part + 1) * ROWS, COLS:]
-                odd = placed[(2 * part + 1) * ROWS : (2 * part + 2) * ROWS, COLS:]
-                side_send[c, part, p] = (even + pltpu.roll(odd, 64, 1)).astype(BF16)
+                second = placed[(2 * part + 1) * ROWS : (2 * part + 2) * ROWS, COLS:]
+                side_send[c, part, p] = (even + pltpu.roll(second, 64, 1)).astype(BF16)
+            if 2 * p < NZ - RELAY:
+                lower_copy(c, slice(2 * p, 2 * p + 2)).start()
+            else:
+
+                @pl.when(odd)
+                def _():
+                    relay_copy(c, 0).start()
+
+                @pl.when(jnp.logical_not(odd))
+                def _():
+                    far_copy(c).start()
+
         start(join_copies(c))
+
+    psf_load.wait()
 
     @pl.loop(0, CH)
     def _(c):
@@ -327,6 +373,18 @@
                 ).astype(BF16)
                 mat_zy[d, c, at_rows, 5 * LANES :] = (y_below * depth_edge[d][z : z + 1]).astype(BF16)
 
+        @pl.when(odd)
+        def _():
+            relay_copy(c, 0).wait_recv()
+            relay_copy(c, 1).start()
+
+    @pl.when(odd)
+    def _():
+        @pl.loop(0, CH)
+        def _(c):
+            relay_copy(c, 1).wait_recv()
+            relay_copy(c, 2).start()
+
     for copy in info_copies():
         copy.wait_recv()
     has_west = jnp.where(gx > 0, 1.0, 0.0).astype(F32)
@@ -368,7 +426,7 @@
 
     @pl.loop(0, CH)
     def _(c):
-        for copy in join_copies(c):
+        for copy in [lower_copy(c), far_copy(c), *join_copies(c)]:
             copy.wait_recv()
         for z in range(NZ):
             total = own[c, z].astype(F32) + has_north * low_recv[c, z].astype(F32)
@@ -431,19 +489,16 @@
             for copy in row_copies(s, c) + edge_copies(s, c):
                 copy.wait_recv()
             blur(d, s, c)
-            for z in range(0, NZ, GROUP):
-                planes = slice(z, z + GROUP)
-                seen = dot(mat_zy[d, c, z * ROWS : (z + GROUP) * ROWS], spread[...])
-                seen = seen.reshape(GROUP, ROWS, COLS)
-                if d == 0:
-                    value = joined[c, planes] / seen
-                else:
-                    value = est_ref[c, planes] * seen
-                    est_ref[c, planes] = value
-                cur[s + 1, c, planes] = value.astype(BF16)
-                start(row_copies(s + 1, c, planes, rows))
+            seen = dot(mat_zy[d, c], spread[...]).reshape(NZ, ROWS, COLS)
+            if d == 0:
+                value = joined[c] / seen
+            else:
+                value = est_ref[c] * seen
+                est_ref[c] = value
+            cur[s + 1, c] = value.astype(BF16)
             pack_edges(s + 1, c, lambda z: cur[s + 1, c, z].astype(F32))
             start(edge_copies(s + 1, c, rows))
+            start(row_copies(s + 1, c, rows))
 
     @pl.loop(0, ITERS - 1)
     def _(it):
@@ -461,7 +516,7 @@
 
     @pl.loop(0, CH)
     def _(c):
-        for copy in row_copies(last, c, rows=EDGE // 2) + edge_copies(last, c, EDGE // 2):
+        for copy in row_copies(last, c, EDGE // 2) + edge_copies(last, c, EDGE // 2):
             copy.wait_recv()
         unpack_edges(last, c)
         main = jnp.zeros((rows_of.shape[0], COLS), F32)
@@ -481,21 +536,32 @@
 
     @pl.loop(0, CH)
     def _(c):
-        for copy in join_copies(c):
+        for copy in [lower_copy(c), *join_copies(c)]:
             copy.wait_send()
+
+        @pl.when(odd)
+        def _():
+            for hop in range(3):
+                relay_copy(c, hop).wait_send()
+
+        @pl.when(jnp.logical_not(odd))
+        def _():
+            far_copy(c).wait_send()
 
         @pl.loop(0, last)
         def _(s):
             for copy in row_copies(s, c) + edge_copies(s, c):
                 copy.wait_send()
 
-        for copy in row_copies(last, c, rows=EDGE // 2) + edge_copies(last, c, EDGE // 2):
+        for copy in row_copies(last, c, EDGE // 2) + edge_copies(last, c, EDGE // 2):
             copy.wait_send()
 
 
 def _settle(*refs):
     sem = refs[-1]
-    copies = [pltpu.make_async_copy(refs[n], refs[n + 3], sem.at[n]) for n in range(3)]
+    pairs = [(refs[0].at[c, z], refs[3].at[c, z]) for c in range(CH) for z in (pl.ds(0, 4), pl.ds(4, 4))]
+    pairs += [(refs[1], refs[4]), (refs[2], refs[5])]
+    copies = [pltpu.make_async_copy(src, dst, sem.at[n]) for n, (src, dst) in enumerate(pairs)]
     for copy in copies:
         copy.start()
     for copy in copies:
@@ -507,7 +573,6 @@
     sizes = (mesh.shape["gx"], mesh.shape["gy"])
     prow = _pyramid_rows()
     pone, ptwo = _pyramid_cols()
-    smem = pl.BlockSpec(memory_space=pltpu.SMEM)
     vmem = pl.BlockSpec(memory_space=pltpu.VMEM)
     hbm = pl.BlockSpec(memory_space=pltpu.HBM)
     dma = pltpu.SemaphoreType.DMA
@@ -520,9 +585,11 @@
                 pltpu.VMEM((CH, NZ // 2, ROWS // 2, COLS // 2), F32),
                 pltpu.VMEM((CH, NZ // 4, ROWS // 4, COLS // 4), F32),
             ),
-            in_specs=[smem, smem, hbm, hbm, hbm, hbm],
+            in_specs=[hbm, hbm, hbm, hbm, hbm, hbm],
             out_specs=(vmem, vmem, vmem),
             scratch_shapes=[
+                pltpu.SMEM((1, 1, 2), jnp.int32),
+                pltpu.SMEM((CH, 3, TAPS), F32),
                 pltpu.VMEM((CH, NZ, TROWS, TCOLS), BF16),
                 pltpu.VMEM(prow.shape, BF16),
                 pltpu.VMEM(pone.shape, BF16),
@@ -547,7 +614,10 @@
                 pltpu.VMEM((ALL, COLS), BF16),
                 pltpu.VMEM((2, CH, COLS, COLS // 2), BF16),
                 pltpu.VMEM((2, CH, OWN, ALL), BF16),
-                dma((CH + 3,)),
+                dma((CH + 5,)),
+                dma((CH, 3)),
+                dma((CH, 3)),
+                pltpu.VMEM((CH, 2, RELAY, ROWS, COLS), BF16),
                 dma((CH, 3)),
                 dma((CH, 3)),
                 dma((3,)),
@@ -567,7 +637,7 @@
             out_shape=tuple(jax.ShapeDtypeStruct(o.shape, o.dtype) for o in outs),
             in_specs=[vmem] * 3,
             out_specs=(hbm,) * 3,
-            scratch_shapes=[dma((3,))],
+            scratch_shapes=[dma((2 * CH + 2,))],
             compiler_params=pltpu.CompilerParams(vmem_limit_bytes=4 * 1024 * 1024),
         )(*[pltpu.with_memory_space_constraint(o, pltpu.VMEM) for o in outs])
 

time: 68.2 us -> 62.9 us (0.922)
  Pallas kernels: 67.4 us -> 62.1 us
    pallas_call x1, Pallas kernels: 65.6 us -> 60.3 us  [per_device(): pl.pallas_call(functools.partial(_kernel, sizes), out_shape=(pltpu.VMEM((...]
where the time goes in v2:
time: 62.9 us; the launch traced here: 62.8 us
  Pallas kernels  62.1 us (99%)
  between operations  0.64 us (1%)
    pallas_call x1, Pallas kernels, per_device(): pl.pallas_call(functools.partial(_kernel, sizes), out_shape=(pltpu.VMEM((...  60.3 us
    pallas_call x1, Pallas kernels, per_device(): pl.pallas_call(_settle, out_shape=tuple((jax.ShapeDtypeStruct(o.shape, o....  1.86 us

profile of v2, /device:TPU:1, one launch (start us, length us, event | category | flops | bytes accessed | tf_op | source)
XLA Modules:
  0.0 62.8 jit_solution(3599205627432561157)
XLA Ops:
  0.6 60.3 %shard_map.85 = (f32[3,8,64,512]{3,2,1,0:T(8,128)S(1)}, f32[3,4,32,256]{3,2,1,0:T(8,128)S(1)}, f32[3,2,16,128]{3,2,1,0:T(8,128)S(1)}) custom-call(s32[1,1,2]{2,1,0:T(1,128)} %offsets_in.1, f32[3,3,31]{2,1,0:T(4,128)} %psf_in.1, bf16[3,8,96,544]{3,2,1,0:T(8,128)(2,1)} %tiles_ref.1, bf16[3,160,768]{2,1,0:T(8,128)(2,1)} %constant.6.clone.prow_ref, ...), custom_call_target="tpu_custom_call" | custom-call | tf_op jit(solution)/shard_map/pallas_call | solution.py:581
  60.9 1.9 %shard_map.86 = (f32[3,8,64,512]{3,2,1,0:T(8,128)}, f32[3,4,32,256]{3,2,1,0:T(8,128)}, f32[3,2,16,128]{3,2,1,0:T(8,128)}) custom-call(f32[3,8,64,512]{3,2,1,0:T(8,128)S(1)} %get-tuple-element.6.refs_0_, f32[3,4,32,256]{3,2,1,0:T(8,128)S(1)} %get-tuple-element.7.refs_1_, f32[3,2,16,128]{3,2,1,0:T(8,128)S(1)} %get-tuple-element.8.refs_2_), custom_call_target="tpu_custom_call" | custom-call | tf_op jit(solution)/shard_map/pallas_call | solution.py:635

commit v3 on v2

--- a/solution.py
+++ b/solution.py
@@ -230,12 +230,12 @@
         upper, lower = pl.ds(ROWS + EDGE - rows, rows), pl.ds(ROWS + EDGE, rows)
         right, left = pack_right.at[s, c], pack_left.at[s, c]
         parts = [
-            (right, left_recv.at[s, c, main], around[0]),
-            (left, right_recv.at[s, c, main], around[1]),
             (pack_right.at[s, c, last], left_recv.at[s, c, upper], around[4]),
             (pack_right.at[s, c, first], left_recv.at[s, c, lower], around[5]),
             (pack_left.at[s, c, last], right_recv.at[s, c, upper], around[6]),
             (pack_left.at[s, c, first], right_recv.at[s, c, lower], around[7]),
+            (right, left_recv.at[s, c, main], around[0]),
+            (left, right_recv.at[s, c, main], around[1]),
         ]
         return [
             remote(src, dst, send_sem.at[s, c, 2 + n], recv_sem.at[s, c, 2 + n], place)
@@ -277,17 +277,16 @@
         side_recv_ref[STEPS - 1, :, ROWS : ROWS + EDGE // 2] = unused
         side_recv_ref[STEPS - 1, :, ROWS + EDGE + EDGE // 2 :] = unused
 
-    pl.semaphore_wait(barrier, len(around) + len(ring))
-    start(info_copies())
-
-    @pl.loop(0, CH)
-    def _(c):
+
+    pairs = (NZ // 2 - 1, *range(NZ // 2 - 1))
+
+    def place_tile(c, then):
         pltpu.make_async_copy(tiles_ref.at[c], tiles_in.at[c], load_sem.at[c]).wait()
         tile = tiles_in[c].reshape(NZ * TROWS, TCOLS)
         shifted[:, 0:half] = dot(tile[:, 0:half], shift_a).astype(BF16)
         shifted[:, half:COLS] = dot(tile[:, LANES:COLS], shift_b).astype(BF16)
         shifted[:, COLS:] = dot(tile[:, COLS - LANES :], shift_c).astype(BF16)
-        for p in (NZ // 2 - 1, *range(NZ // 2 - 1)):
+        for p in pairs:
             placed = dot(lower_it, shifted[2 * p * TROWS : 2 * (p + 1) * TROWS, :])
             for zz in range(2):
                 own[c, 2 * p + zz] = placed[zz * ROWS : (zz + 1) * ROWS, :COLS].astype(BF16)
@@ -296,18 +295,31 @@
                 even = placed[2 * part * ROWS : (2 * part + 1) * ROWS, COLS:]
                 second = placed[(2 * part + 1) * ROWS : (2 * part + 2) * ROWS, COLS:]
                 side_send[c, part, p] = (even + pltpu.roll(second, 64, 1)).astype(BF16)
-            if 2 * p < NZ - RELAY:
-                lower_copy(c, slice(2 * p, 2 * p + 2)).start()
-            else:
-
-                @pl.when(odd)
-                def _():
-                    relay_copy(c, 0).start()
-
-                @pl.when(jnp.logical_not(odd))
-                def _():
-                    far_copy(c).start()
-
+            then(p)
+
+    def send_rows(c, p):
+        if 2 * p < NZ - RELAY:
+            lower_copy(c, slice(2 * p, 2 * p + 2)).start()
+        else:
+
+            @pl.when(odd)
+            def _():
+                relay_copy(c, 0).start()
+
+            @pl.when(jnp.logical_not(odd))
+            def _():
+                far_copy(c).start()
+
+    place_tile(0, lambda p: None)
+    pl.semaphore_wait(barrier, len(around) + len(ring))
+    start(info_copies())
+    for p in pairs:
+        send_rows(0, p)
+    start(join_copies(0))
+
+    @pl.loop(1, CH)
+    def _(c):
+        place_tile(c, lambda p: send_rows(c, p))
         start(join_copies(c))
 
     psf_load.wait()
@@ -441,9 +453,9 @@
             joined[c, z] = value
             est_ref[c, z] = value
             cur[0, c, z] = value.astype(BF16)
-        start(row_copies(0, c))
         pack_edges(0, c, lambda z: joined[c, z])
         start(edge_copies(0, c))
+        start(row_copies(0, c))
 
     wide_lane = _iota((ROWS + 2 * EDGE, LANES), 1)
     from_west = (wide_lane >= LANES - EDGE) & (gx > 0)

time: 62.9 us -> 60.9 us (0.968)
  Pallas kernels: 62.1 us -> 60.1 us
    pallas_call x1, Pallas kernels: 60.3 us -> 58.3 us  [per_device(): pl.pallas_call(functools.partial(_kernel, sizes), out_shape=(pltpu.VMEM((...]
where the time goes in v3:
time: 60.9 us; the launch traced here: 60.8 us
  Pallas kernels  60.1 us (99%)
  between operations  0.64 us (1%)
    pallas_call x1, Pallas kernels, per_device(): pl.pallas_call(functools.partial(_kernel, sizes), out_shape=(pltpu.VMEM((...  58.3 us
    pallas_call x1, Pallas kernels, per_device(): pl.pallas_call(_settle, out_shape=tuple((jax.ShapeDtypeStruct(o.shape, o....  1.86 us

profile of v3, /device:TPU:1, one launch (start us, length us, event | category | flops | bytes accessed | tf_op | source)
XLA Modules:
  0.0 60.8 jit_solution(9627372918167496150)
XLA Ops:
  0.6 58.3 %shard_map.85 = (f32[3,8,64,512]{3,2,1,0:T(8,128)S(1)}, f32[3,4,32,256]{3,2,1,0:T(8,128)S(1)}, f32[3,2,16,128]{3,2,1,0:T(8,128)S(1)}) custom-call(s32[1,1,2]{2,1,0:T(1,128)} %offsets_in.1, f32[3,3,31]{2,1,0:T(4,128)} %psf_in.1, bf16[3,8,96,544]{3,2,1,0:T(8,128)(2,1)} %tiles_ref.1, bf16[3,160,768]{2,1,0:T(8,128)(2,1)} %constant.6.clone.prow_ref, ...), custom_call_target="tpu_custom_call" | custom-call | tf_op jit(solution)/shard_map/pallas_call | solution.py:593
  58.9 1.9 %shard_map.86 = (f32[3,8,64,512]{3,2,1,0:T(8,128)}, f32[3,4,32,256]{3,2,1,0:T(8,128)}, f32[3,2,16,128]{3,2,1,0:T(8,128)}) custom-call(f32[3,8,64,512]{3,2,1,0:T(8,128)S(1)} %get-tuple-element.6.refs_0_, f32[3,4,32,256]{3,2,1,0:T(8,128)S(1)} %get-tuple-element.7.refs_1_, f32[3,2,16,128]{3,2,1,0:T(8,128)S(1)} %get-tuple-element.8.refs_2_), custom_call_target="tpu_custom_call" | custom-call | tf_op jit(solution)/shard_map/pallas_call | solution.py:647

commit v4 on v3

--- a/solution.py
+++ b/solution.py
@@ -218,8 +218,8 @@
             remote(
                 cur.at[s, c, :, src],
                 strip_recv.at[s, c, n, :, dst],
-                send_sem.at[s, c, n],
-                recv_sem.at[s, c, n],
+                send_sem.at[c, n],
+                recv_sem.at[s % 2, c, n],
                 place,
             )
             for src, n, dst, place in parts
@@ -238,7 +238,7 @@
             (left, right_recv.at[s, c, main], around[1]),
         ]
         return [
-            remote(src, dst, send_sem.at[s, c, 2 + n], recv_sem.at[s, c, 2 + n], place)
+            remote(src, dst, send_sem.at[c, 2 + n], recv_sem.at[s % 2, c, 2 + n], place)
             for n, (src, dst, place) in enumerate(parts)
         ]
 
@@ -509,16 +509,34 @@
                 est_ref[c] = value
             cur[s + 1, c] = value.astype(BF16)
             pack_edges(s + 1, c, lambda z: cur[s + 1, c, z].astype(F32))
+            for copy in edge_copies(s, c) + row_copies(s, c):
+                copy.wait_send()
             start(edge_copies(s + 1, c, rows))
             start(row_copies(s + 1, c, rows))
 
-    @pl.loop(0, ITERS - 1)
-    def _(it):
+    def join_sent():
+        for copy in info_copies():
+            copy.wait_send()
+
+        @pl.loop(0, CH)
+        def _(c):
+            for copy in [lower_copy(c), *join_copies(c)]:
+                copy.wait_send()
+
+            @pl.when(odd)
+            def _():
+                for hop in range(3):
+                    relay_copy(c, hop).wait_send()
+
+            @pl.when(jnp.logical_not(odd))
+            def _():
+                far_copy(c).wait_send()
+
+    for it in range(ITERS):
         iterate(it, 0, False)
-        iterate(it, 1, False)
-
-    iterate(ITERS - 1, 0, False)
-    iterate(ITERS - 1, 1, True)
+        if it == 0:
+            join_sent()
+        iterate(it, 1, it == ITERS - 1)
 
     for copy in constant_loads:
         copy.wait()
@@ -542,32 +560,8 @@
         one_ref[c] = one.reshape(NZ // 2, ROWS // 2, COLS // 2)
         two = dot(high[n_one:], cols_of) + dot(low[n_one:], cols_of)
         two_ref[c] = two.reshape(NZ // 4, ROWS // 4, COLS // 4)
-
-    for copy in info_copies():
-        copy.wait_send()
-
-    @pl.loop(0, CH)
-    def _(c):
-        for copy in [lower_copy(c), *join_copies(c)]:
-            copy.wait_send()
-
-        @pl.when(odd)
-        def _():
-            for hop in range(3):
-                relay_copy(c, hop).wait_send()
-
-        @pl.when(jnp.logical_not(odd))
-        def _():
-            far_copy(c).wait_send()
-
-        @pl.loop(0, last)
-        def _(s):
-            for copy in row_copies(s, c) + edge_copies(s, c):
-                copy.wait_send()
-
         for copy in row_copies(last, c, EDGE // 2) + edge_copies(last, c, EDGE // 2):
             copy.wait_send()
-
 
 def _settle(*refs):
     sem = refs[-1]
@@ -634,8 +628,8 @@
                 dma((CH, 3)),
                 dma((3,)),
                 dma((3,)),
-                dma((STEPS, CH, 8)),
-                dma((STEPS, CH, 8)),
+                dma((CH, 8)),
+                dma((2, CH, 8)),
             ],
             compiler_params=pltpu.CompilerParams(
                 collective_id=0, has_side_effects=True, vmem_limit_bytes=48 * 1024 * 1024

time: 60.9 us -> 59.2 us (0.972)
  Pallas kernels: 60.1 us -> 58.5 us
    pallas_call x1, Pallas kernels: 58.3 us -> 56.6 us  [per_device(): pl.pallas_call(functools.partial(_kernel, sizes), out_shape=(pltpu.VMEM((...]
where the time goes in v4:
time: 59.2 us; the launch traced here: 59.1 us
  Pallas kernels  58.5 us (99%)
  between operations  0.64 us (1%)
    pallas_call x1, Pallas kernels, per_device(): pl.pallas_call(functools.partial(_kernel, sizes), out_shape=(pltpu.VMEM((...  56.6 us
    pallas_call x1, Pallas kernels, per_device(): pl.pallas_call(_settle, out_shape=tuple((jax.ShapeDtypeStruct(o.shape, o....  1.86 us

profile of v4, /device:TPU:1, one launch (start us, length us, event | category | flops | bytes accessed | tf_op | source)
XLA Modules:
  0.0 59.1 jit_solution(18417533058067160799)
XLA Ops:
  0.6 56.6 %shard_map.85 = (f32[3,8,64,512]{3,2,1,0:T(8,128)S(1)}, f32[3,4,32,256]{3,2,1,0:T(8,128)S(1)}, f32[3,2,16,128]{3,2,1,0:T(8,128)S(1)}) custom-call(s32[1,1,2]{2,1,0:T(1,128)} %offsets_in.1, f32[3,3,31]{2,1,0:T(4,128)} %psf_in.1, bf16[3,8,96,544]{3,2,1,0:T(8,128)(2,1)} %tiles_ref.1, bf16[3,160,768]{2,1,0:T(8,128)(2,1)} %constant.6.clone.prow_ref, ...), custom_call_target="tpu_custom_call" | custom-call | tf_op jit(solution)/shard_map/pallas_call | solution.py:587
  57.2 1.9 %shard_map.86 = (f32[3,8,64,512]{3,2,1,0:T(8,128)}, f32[3,4,32,256]{3,2,1,0:T(8,128)}, f32[3,2,16,128]{3,2,1,0:T(8,128)}) custom-call(f32[3,8,64,512]{3,2,1,0:T(8,128)S(1)} %get-tuple-element.6.refs_0_, f32[3,4,32,256]{3,2,1,0:T(8,128)S(1)} %get-tuple-element.7.refs_1_, f32[3,2,16,128]{3,2,1,0:T(8,128)S(1)} %get-tuple-element.8.refs_2_), custom_call_target="tpu_custom_call" | custom-call | tf_op jit(solution)/shard_map/pallas_call | solution.py:641

commit v5 on v4

--- a/solution.py
+++ b/solution.py
@@ -165,8 +165,8 @@
     ]
     offsets_load = pltpu.make_async_copy(offsets_in, offsets_ref, load_sem.at[CH + 3])
     psf_load = pltpu.make_async_copy(psf_in, psf_ref, load_sem.at[CH + 4])
-    for copy in [offsets_load, *tile_loads, psf_load, *constant_loads]:
-        copy.start()
+    offsets_load.start()
+    tile_loads[0].start()
 
     def remote(src, dst, send, recv, place):
         return pltpu.make_async_remote_copy(
@@ -219,7 +219,7 @@
                 cur.at[s, c, :, src],
                 strip_recv.at[s, c, n, :, dst],
                 send_sem.at[c, n],
-                recv_sem.at[s % 2, c, n],
+                recv_sem.at[s % 2, c, 0],
                 place,
             )
             for src, n, dst, place in parts
@@ -230,17 +230,24 @@
         upper, lower = pl.ds(ROWS + EDGE - rows, rows), pl.ds(ROWS + EDGE, rows)
         right, left = pack_right.at[s, c], pack_left.at[s, c]
         parts = [
-            (pack_right.at[s, c, last], left_recv.at[s, c, upper], around[4]),
-            (pack_right.at[s, c, first], left_recv.at[s, c, lower], around[5]),
-            (pack_left.at[s, c, last], right_recv.at[s, c, upper], around[6]),
-            (pack_left.at[s, c, first], right_recv.at[s, c, lower], around[7]),
-            (right, left_recv.at[s, c, main], around[0]),
-            (left, right_recv.at[s, c, main], around[1]),
+            (pack_right.at[s, c, last], left_recv.at[s, c, upper], around[4], 1),
+            (pack_right.at[s, c, first], left_recv.at[s, c, lower], around[5], 1),
+            (pack_left.at[s, c, last], right_recv.at[s, c, upper], around[6], 2),
+            (pack_left.at[s, c, first], right_recv.at[s, c, lower], around[7], 2),
+            (right, left_recv.at[s, c, main], around[0], 1),
+            (left, right_recv.at[s, c, main], around[1], 2),
         ]
         return [
-            remote(src, dst, send_sem.at[c, 2 + n], recv_sem.at[s % 2, c, 2 + n], place)
-            for n, (src, dst, place) in enumerate(parts)
+            remote(src, dst, send_sem.at[c, 2 + n], recv_sem.at[s % 2, c, side], place)
+            for n, (src, dst, place, side) in enumerate(parts)
         ]
+
+    def arrived(s, c, rows=EDGE):
+        near, side = pl.ds(0, rows), pl.ds(0, ROWS + 2 * rows)
+        for n, ref in enumerate(
+            (strip_recv.at[s, c, :, :, near], left_recv.at[s, c, side], right_recv.at[s, c, side])
+        ):
+            remote(ref, ref, send_sem.at[c, n], recv_sem.at[s % 2, c, n], around[0]).wait_recv()
 
     def start(copies):
         for copy in copies:
@@ -311,6 +318,8 @@
                 far_copy(c).start()
 
     place_tile(0, lambda p: None)
+    for copy in [*tile_loads[1:], psf_load, *constant_loads]:
+        copy.start()
     pl.semaphore_wait(barrier, len(around) + len(ring))
     start(info_copies())
     for p in pairs:
@@ -498,8 +507,7 @@
 
         @pl.loop(0, CH)
         def _(c):
-            for copy in row_copies(s, c) + edge_copies(s, c):
-                copy.wait_recv()
+            arrived(s, c)
             blur(d, s, c)
             seen = dot(mat_zy[d, c], spread[...]).reshape(NZ, ROWS, COLS)
             if d == 0:
@@ -546,8 +554,7 @@
 
     @pl.loop(0, CH)
     def _(c):
-        for copy in row_copies(last, c, EDGE // 2) + edge_copies(last, c, EDGE // 2):
-            copy.wait_recv()
+        arrived(last, c, EDGE // 2)
         unpack_edges(last, c)
         main = jnp.zeros((rows_of.shape[0], COLS), F32)
         for begin, size, field in segments(last, c):
@@ -629,7 +636,7 @@
                 dma((3,)),
                 dma((3,)),
                 dma((CH, 8)),
-                dma((2, CH, 8)),
+                dma((2, CH, 3)),
             ],
             compiler_params=pltpu.CompilerParams(
                 collective_id=0, has_side_effects=True, vmem_limit_bytes=48 * 1024 * 1024

time: 59.2 us -> 59 us (level)
  no operation moved by 1% of the time
where the time goes in v5:
time: 59 us; the launch traced here: 58.8 us
  Pallas kernels  58.2 us (99%)
  between operations  0.64 us (1%)
    pallas_call x1, Pallas kernels, per_device(): pl.pallas_call(functools.partial(_kernel, sizes), out_shape=(pltpu.VMEM((...  56.3 us
    pallas_call x1, Pallas kernels, per_device(): pl.pallas_call(_settle, out_shape=tuple((jax.ShapeDtypeStruct(o.shape, o....  1.86 us

profile of v5, /device:TPU:1, one launch (start us, length us, event | category | flops | bytes accessed | tf_op | source)
XLA Modules:
  0.0 58.8 jit_solution(1150593865252782721)
XLA Ops:
  0.6 56.3 %shard_map.85 = (f32[3,8,64,512]{3,2,1,0:T(8,128)S(1)}, f32[3,4,32,256]{3,2,1,0:T(8,128)S(1)}, f32[3,2,16,128]{3,2,1,0:T(8,128)S(1)}) custom-call(s32[1,1,2]{2,1,0:T(1,128)} %offsets_in.1, f32[3,3,31]{2,1,0:T(4,128)} %psf_in.1, bf16[3,8,96,544]{3,2,1,0:T(8,128)(2,1)} %tiles_ref.1, bf16[3,160,768]{2,1,0:T(8,128)(2,1)} %constant.6.clone.prow_ref, ...), custom_call_target="tpu_custom_call" | custom-call | tf_op jit(solution)/shard_map/pallas_call | solution.py:594
  57.0 1.9 %shard_map.86 = (f32[3,8,64,512]{3,2,1,0:T(8,128)}, f32[3,4,32,256]{3,2,1,0:T(8,128)}, f32[3,2,16,128]{3,2,1,0:T(8,128)}) custom-call(f32[3,8,64,512]{3,2,1,0:T(8,128)S(1)} %get-tuple-element.6.refs_0_, f32[3,4,32,256]{3,2,1,0:T(8,128)S(1)} %get-tuple-element.7.refs_1_, f32[3,2,16,128]{3,2,1,0:T(8,128)S(1)} %get-tuple-element.8.refs_2_), custom_call_target="tpu_custom_call" | custom-call | tf_op jit(solution)/shard_map/pallas_call | solution.py:648

commit v6 on v4

--- a/solution.py
+++ b/solution.py
@@ -120,10 +120,8 @@
     mat_x,
     mat_zy,
     load_sem,
-    join_send_sem,
     join_recv_sem,
     relay,
-    relay_send_sem,
     relay_recv_sem,
     info_send_sem,
     info_recv_sem,
@@ -175,21 +173,21 @@
 
     def join_copies(c):
         return [
-            remote(side_send.at[c, 0], side_recv.at[c, 0], join_send_sem.at[c, 1], join_recv_sem.at[c, 1], around[0]),
-            remote(side_send.at[c, 1], side_recv.at[c, 1], join_send_sem.at[c, 2], join_recv_sem.at[c, 2], around[4]),
+            remote(side_send.at[c, 0], side_recv.at[c, 0], send_sem.at[c, 1], join_recv_sem.at[c, 1], around[0]),
+            remote(side_send.at[c, 1], side_recv.at[c, 1], send_sem.at[c, 2], join_recv_sem.at[c, 2], around[4]),
         ]
 
     def lower_copy(c, planes=slice(0, NZ - RELAY)):
         z = pl.ds(planes.start, planes.stop - planes.start)
         return remote(
-            low_send.at[c, z], low_recv.at[c, z], join_send_sem.at[c, 0], join_recv_sem.at[c, 0], around[2]
+            low_send.at[c, z], low_recv.at[c, z], send_sem.at[c, 0], join_recv_sem.at[c, 0], around[2]
         )
 
     far = pl.ds(NZ - RELAY, RELAY)
 
     def far_copy(c):
         return remote(
-            low_send.at[c, far], low_recv.at[c, far], relay_send_sem.at[c, 0], relay_recv_sem.at[c, 0], around[2]
+            low_send.at[c, far], low_recv.at[c, far], send_sem.at[c, 3], relay_recv_sem.at[c, 0], around[2]
         )
 
     def relay_copy(c, hop):
@@ -198,7 +196,7 @@
         return remote(
             src,
             dst,
-            relay_send_sem.at[c, hop],
+            send_sem.at[c, 3 + hop],
             relay_recv_sem.at[c, 0 if hop == 2 else hop + 1],
             ring[1] if hop == 2 else ring[0],
         )
@@ -454,6 +452,18 @@
             est_ref[c, z] = value
             cur[0, c, z] = value.astype(BF16)
         pack_edges(0, c, lambda z: joined[c, z])
+        for copy in [lower_copy(c), *join_copies(c)]:
+            copy.wait_send()
+
+        @pl.when(odd)
+        def _():
+            for hop in range(3):
+                relay_copy(c, hop).wait_send()
+
+        @pl.when(jnp.logical_not(odd))
+        def _():
+            far_copy(c).wait_send()
+
         start(edge_copies(0, c))
         start(row_copies(0, c))
 
@@ -514,29 +524,12 @@
             start(edge_copies(s + 1, c, rows))
             start(row_copies(s + 1, c, rows))
 
-    def join_sent():
-        for copy in info_copies():
-            copy.wait_send()
-
-        @pl.loop(0, CH)
-        def _(c):
-            for copy in [lower_copy(c), *join_copies(c)]:
-                copy.wait_send()
-
-            @pl.when(odd)
-            def _():
-                for hop in range(3):
-                    relay_copy(c, hop).wait_send()
-
-            @pl.when(jnp.logical_not(odd))
-            def _():
-                far_copy(c).wait_send()
-
     for it in range(ITERS):
         iterate(it, 0, False)
-        if it == 0:
-            join_sent()
         iterate(it, 1, it == ITERS - 1)
+
+    for copy in info_copies():
+        copy.wait_send()
 
     for copy in constant_loads:
         copy.wait()
@@ -565,8 +558,7 @@
 
 def _settle(*refs):
     sem = refs[-1]
-    pairs = [(refs[0].at[c, z], refs[3].at[c, z]) for c in range(CH) for z in (pl.ds(0, 4), pl.ds(4, 4))]
-    pairs += [(refs[1], refs[4]), (refs[2], refs[5])]
+    pairs = [(refs[n], refs[n + 3]) for n in range(3)]
     copies = [pltpu.make_async_copy(src, dst, sem.at[n]) for n, (src, dst) in enumerate(pairs)]
     for copy in copies:
         copy.start()
@@ -622,9 +614,7 @@
                 pltpu.VMEM((2, CH, OWN, ALL), BF16),
                 dma((CH + 5,)),
                 dma((CH, 3)),
-                dma((CH, 3)),
                 pltpu.VMEM((CH, 2, RELAY, ROWS, COLS), BF16),
-                dma((CH, 3)),
                 dma((CH, 3)),
                 dma((3,)),
                 dma((3,)),
@@ -643,7 +633,7 @@
             out_shape=tuple(jax.ShapeDtypeStruct(o.shape, o.dtype) for o in outs),
             in_specs=[vmem] * 3,
             out_specs=(hbm,) * 3,
-            scratch_shapes=[dma((2 * CH + 2,))],
+            scratch_shapes=[dma((3,))],
             compiler_params=pltpu.CompilerParams(vmem_limit_bytes=4 * 1024 * 1024),
         )(*[pltpu.with_memory_space_constraint(o, pltpu.VMEM) for o in outs])
 

time: 59.2 us -> 59 us (level)
  no operation moved by 1% of the time
where the time goes in v6:
time: 59 us; the launch traced here: 58.9 us
  Pallas kernels  58.2 us (99%)
  between operations  0.64 us (1%)
    pallas_call x1, Pallas kernels, per_device(): pl.pallas_call(functools.partial(_kernel, sizes), out_shape=(pltpu.VMEM((...  56.4 us
    pallas_call x1, Pallas kernels, per_device(): pl.pallas_call(_settle, out_shape=tuple((jax.ShapeDtypeStruct(o.shape, o....  1.81 us

profile of v6, /device:TPU:1, one launch (start us, length us, event | category | flops | bytes accessed | tf_op | source)
XLA Modules:
  0.0 58.9 jit_solution(12447024964775298027)
XLA Ops:
  0.6 56.4 %shard_map.85 = (f32[3,8,64,512]{3,2,1,0:T(8,128)S(1)}, f32[3,4,32,256]{3,2,1,0:T(8,128)S(1)}, f32[3,2,16,128]{3,2,1,0:T(8,128)S(1)}) custom-call(s32[1,1,2]{2,1,0:T(1,128)} %offsets_in.1, f32[3,3,31]{2,1,0:T(4,128)} %psf_in.1, bf16[3,8,96,544]{3,2,1,0:T(8,128)(2,1)} %tiles_ref.1, bf16[3,160,768]{2,1,0:T(8,128)(2,1)} %constant.6.clone.prow_ref, ...), custom_call_target="tpu_custom_call" | custom-call | tf_op jit(solution)/shard_map/pallas_call | solution.py:579
  57.1 1.8 %shard_map.86 = (f32[3,8,64,512]{3,2,1,0:T(8,128)}, f32[3,4,32,256]{3,2,1,0:T(8,128)}, f32[3,2,16,128]{3,2,1,0:T(8,128)}) custom-call(f32[3,8,64,512]{3,2,1,0:T(8,128)S(1)} %get-tuple-element.6.refs_0_, f32[3,4,32,256]{3,2,1,0:T(8,128)S(1)} %get-tuple-element.7.refs_1_, f32[3,2,16,128]{3,2,1,0:T(8,128)S(1)} %get-tuple-element.8.refs_2_), custom_call_target="tpu_custom_call" | custom-call | tf_op jit(solution)/shard_map/pallas_call | solution.py:631
